TPU v7x, 256 devices: a whole 4x4x8 slice. The times are simulated.
256 devices in a mesh: row: 8 (over z_hi, x), col: 32 (over z_lo, y, core).
Axes of the slice: x: 4, y: 4, z: 8 (z_hi: 2, z_lo: 4; z = z_hi * 4 + z_lo), core: 2. Of those that a mesh axis runs over, the one named last changes fastest.
Arguments:
- contexts: bfloat16 [32768, 128], P(('row', 'col')), may hold values from -8 to 8
- logged_actions: int32 [32768], P(('row', 'col')), may hold values from 0 to 131041
- policy_actions: int32 [32768, 8], P(('row', 'col')), may hold values from 0 to 131041
- rewards: float32 [32768], P(('row', 'col')), may hold values from 0.2 to 2
Outputs:
- weights: float32 [32768, 8], P(('row', 'col'))
- residual: float32 [32768, 8], P(('row', 'col'))
- values: float32 [8], replicated
All inputs are finite; a program needn't handle non-finite values.
Results may differ from a plain program's by a relative error of at most 0.0056.
Values may be sent and summed in bfloat16 or wider, within the bound.
No kernel may reach another device: no remote copies, remote signals or barrier semaphores. Data moves between devices by JAX's collectives and lax.ppermute only.
A program may use at most 64 MiB of HBM per device.

v0:
```python
import math
import jax
import jax.numpy as jnp
from jax import lax
from jax.sharding import PartitionSpec as P

NPOL = 8
NACT = 16
CATALOG = 131042
ridge = 0.1
group_size = 16
stride_base = 1009
phase_step = 0.37
two_pi = 2.0 * math.pi


def action_features(chosen, width):
    levels = jnp.arange(width, dtype=jnp.int32)
    multipliers = 1 + stride_base * levels
    turned = chosen[..., None] * multipliers % CATALOG
    angles = turned.astype(jnp.float32) * (two_pi / CATALOG) + phase_step * levels.astype(
        jnp.float32
    )
    wave_terms = math.sqrt(2.0 / width) * jnp.cos(angles)
    constant_term = jnp.full(wave_terms.shape, 1.0 / math.sqrt(width), jnp.float32)
    return jnp.where(levels == 0, constant_term, wave_terms).astype(jnp.bfloat16)


def select_actions(products, onehot):
    shaped = products.reshape(
        products.shape[:-1] + (products.shape[-1] // onehot.shape[-1], onehot.shape[-1])
    )
    return jnp.sum(shaped * jnp.expand_dims(onehot.astype(jnp.float32), -2), axis=-1)


def kernel_tiles(left_tiles, right_tiles, left_squares, right_squares):
    inner = jnp.einsum("grd,gsd->grs", left_tiles, right_tiles, preferred_element_type=jnp.float32)
    expo = (2.0 * inner - left_squares[:, :, None] - right_squares[:, None, :]) / left_tiles.shape[
        -1
    ]
    return jnp.exp(expo).astype(jnp.bfloat16)


def tile_terms(kernel, left_matrix, right_matrix, left_onehot, right_onehot):
    toward_left = jnp.einsum(
        "grs,gsm->grm", kernel, right_matrix, preferred_element_type=jnp.float32
    )
    toward_right = jnp.einsum(
        "grs,grm->gsm", kernel, left_matrix, preferred_element_type=jnp.float32
    )
    return (select_actions(toward_left, left_onehot), select_actions(toward_right, right_onehot))


def listed_pass(
    left_ctx,
    left_squares,
    left_matrix,
    left_onehot,
    right_ctx,
    right_squares,
    right_matrix,
    right_onehot,
    placed,
    diagonal,
):
    left_count = left_ctx.shape[0]
    tile_rows = left_ctx.shape[1]
    right_count = right_ctx.shape[0]
    policies = left_matrix.shape[-1] // left_onehot.shape[-1]
    flat_placed = placed.reshape(-1)
    flat_diagonal = diagonal.reshape(-1)
    plan = jnp.argsort(1 - flat_placed, stable=True)
    active_count = jnp.sum(flat_placed)
    rounds = (active_count + group_size - 1) // group_size

    def advance(round_index, carried):
        row_sums, column_sums = carried
        picked = lax.dynamic_slice_in_dim(plan, round_index * group_size, group_size)
        left_pick = picked // right_count
        right_pick = picked % right_count
        live_flags = jnp.take(flat_placed, picked).astype(jnp.float32)
        mirror_flags = live_flags * (1 - jnp.take(flat_diagonal, picked)).astype(jnp.float32)
        kernel = kernel_tiles(
            left_ctx[left_pick],
            right_ctx[right_pick],
            left_squares[left_pick],
            right_squares[right_pick],
        )
        toward_left, toward_right = tile_terms(
            kernel,
            left_matrix[left_pick],
            right_matrix[right_pick],
            left_onehot[left_pick],
            right_onehot[right_pick],
        )
        row_sums = row_sums.at[left_pick].add(toward_left * live_flags[:, None, None])
        column_sums = column_sums.at[right_pick].add(toward_right * mirror_flags[:, None, None])
        return (row_sums, column_sums)

    start_rows = jnp.zeros((left_count, tile_rows, policies), jnp.float32)
    start_columns = jnp.zeros((right_count, tile_rows, policies), jnp.float32)
    return lax.fori_loop(0, rounds, advance, (start_rows, start_columns))


def on_device(contexts, logged_actions, policy_actions, rewards):
    tile_rows, feature_count = contexts.shape
    left_count = lax.axis_size("col")
    right_count = lax.axis_size("row")
    factor = NACT / (tile_rows * left_count * right_count)
    own_column = lax.axis_index("col")
    own_row = lax.axis_index("row")
    left_ids = jnp.arange(left_count, dtype=jnp.int32)[:, None]
    right_ids = jnp.arange(right_count, dtype=jnp.int32)[None, :]
    first_owner = own_row * left_count + left_ids
    second_owner = right_ids * left_count + own_column
    parity = (first_owner + second_owner) % 2
    placed = jnp.where(
        first_owner == second_owner, 1, jnp.where(first_owner < second_owner, parity, 1 - parity)
    )
    diagonal = ((left_ids == own_column) & (right_ids == own_row)).astype(jnp.int32)
    left_logged, left_policy = (
        lax.all_gather(logged_actions, "col", axis=0, tiled=True),
        lax.all_gather(policy_actions, "col", axis=0, tiled=True),
    )
    right_logged, right_policy = (
        lax.all_gather(logged_actions, "row", axis=0, tiled=True),
        lax.all_gather(policy_actions, "row", axis=0, tiled=True),
    )
    left_onehot = action_features(left_logged, NACT).reshape(left_count, tile_rows, NACT)
    right_onehot = action_features(right_logged, NACT).reshape(right_count, tile_rows, NACT)
    left_first = action_features(left_policy, NACT).reshape(left_count, tile_rows, NPOL * NACT)
    right_first = action_features(right_policy, NACT).reshape(right_count, tile_rows, NPOL * NACT)
    right_ctx = lax.all_gather(contexts, "row", axis=0, tiled=True).reshape(
        right_count, tile_rows, feature_count
    )
    right_squares = jnp.sum(right_ctx.astype(jnp.float32) ** 2, axis=2)
    left_ctx = lax.all_gather(contexts, "col", axis=0, tiled=True).reshape(
        left_count, tile_rows, feature_count
    )
    left_squares = jnp.sum(left_ctx.astype(jnp.float32) ** 2, axis=2)

    def sweep(left_matrix, right_matrix):
        return listed_pass(
            left_ctx,
            left_squares,
            left_matrix,
            left_onehot,
            right_ctx,
            right_squares,
            right_matrix,
            right_onehot,
            placed,
            diagonal,
        )

    def reduce_terms(toward_left, toward_right):
        mine_left = lax.psum_scatter(toward_left, "col", scatter_dimension=0, tiled=True)
        mine_right = lax.psum_scatter(toward_right, "row", scatter_dimension=0, tiled=True)
        return factor * (mine_left[0] + mine_right[0])

    first_left, first_right = sweep(left_first, right_first)
    right_side = reduce_terms(first_left, first_right)
    right_low = right_side.astype(jnp.bfloat16)
    left_rhs = lax.all_gather(right_low, "col", axis=0, tiled=True).reshape(
        left_count, tile_rows, NPOL
    )
    right_rhs = lax.all_gather(right_low, "row", axis=0, tiled=True).reshape(
        right_count, tile_rows, NPOL
    )
    left_second = (left_onehot[:, :, None, :] * left_rhs[:, :, :, None]).reshape(
        left_count, tile_rows, NPOL * NACT
    )
    right_second = (right_onehot[:, :, None, :] * right_rhs[:, :, :, None]).reshape(
        right_count, tile_rows, NPOL * NACT
    )
    second_left, second_right = sweep(left_second, right_second)
    image = reduce_terms(second_left, second_right) + ridge * right_side
    norm_sums, curvature, reward_sums = lax.psum(
        (
            jnp.sum(right_side * right_side, axis=0),
            jnp.sum(right_side * image, axis=0),
            jnp.sum(rewards[:, None] * right_side, axis=0),
        ),
        ("row", "col"),
    )
    alpha = norm_sums / curvature
    weights = alpha[None, :] * right_side
    residual = right_side - alpha[None, :] * image
    values = alpha * reward_sums / (tile_rows * left_count * right_count)
    return (weights, residual, values)


def solution(mesh):
    placed = (
        P(("row", "col"), None),
        P(("row", "col")),
        P(("row", "col"), None),
        P(("row", "col")),
    )
    return jax.shard_map(
        on_device,
        mesh=mesh,
        in_specs=placed,
        out_specs=(P(("row", "col"), None), P(("row", "col"), None), P()),
        check_vma=False,
    )
```

profile of v0, /device:TPU:1, one launch (start us, length us, event | category | flops | bytes accessed | tf_op | source)
XLA Modules:
  0.0 1289.7 jit_solution(7908967299347687956)
XLA Ops:
  11.6 3.2 sort.19
  14.8 29.4 %all-gather.1 = s32[8,1,128]{2,1,0:T(1,128)S(1)} all-gather(s32[1,1,128]{2,1,0:T(1,128)} %bitcast.113), channel_id=1, replica_groups=mesh['row'=8,'col'=32] {'row'}, dimensions={0}, use_global_device_ids=true | all-gather | bytes 4608 | tf_op jit(solution)/shard_map/all_gather | solution.py:126
  44.2 46.1 %all-gather = s32[32,1,128]{2,1,0:T(1,128)S(1)} all-gather(s32[1,1,128]{2,1,0:T(1,128)} %bitcast.114), channel_id=1, replica_groups=mesh['row'=8,'col'=32] {'col'}, dimensions={0}, use_global_device_ids=true | all-gather | bytes 16896 | tf_op jit(solution)/shard_map/all_gather | solution.py:122
  90.3 37.4 %all_gather.26 = s32[1024,8]{0,1:T(8,128)S(1)} all-gather(s32[128,8]{0,1:T(8,128)} %param.12), channel_id=1, replica_groups=mesh['row'=8,'col'=32] {'row'}, dimensions={0}, use_global_device_ids=true | all-gather | bytes 36864 | tf_op jit(solution)/shard_map/all_gather | solution.py:127
  127.8 44.6 %all_gather.28 = s32[4096,8]{0,1:T(8,128)S(1)} all-gather(s32[128,8]{0,1:T(8,128)} %param.12), channel_id=1, replica_groups=mesh['row'=8,'col'=32] {'col'}, dimensions={0}, use_global_device_ids=true | all-gather | bytes 135168 | tf_op jit(solution)/shard_map/all_gather | solution.py:123
  173.5 37.9 %all_gather.25 = bf16[1024,128]{1,0:T(8,128)(2,1)S(1)} all-gather(bf16[128,128]{1,0:T(8,128)(2,1)} %param.10), channel_id=1, replica_groups=mesh['row'=8,'col'=32] {'row'}, dimensions={0}, use_global_device_ids=true | all-gather | bytes 294912 | tf_op jit(solution)/shard_map/all_gather | solution.py:133
  212.7 1.8 multiply_reduce_fusion.4
  214.6 266.5 %while.32 = (s32[]{:T(128)}, f32[32,128,8]{1,2,0:T(8,128)S(1)}, f32[8,128,8]{1,2,0:T(8,128)S(1)}, s32[]{:T(128)}, s32[256]{0:T(256)}, /*index=5*/bf16[32,128,128...) while((s32[]{:T(128)}, f32[32,128,8]{1,2,0:T(8,128)S(1)}, ...), condition=%wide.region_9.11_spmd.clone.clone, body=%wide.region_4.10_spmd.clone.clone.sunk | while | flops 213377504 | bytes 27038416 | solution.py:102
  217.6 1.9 gather_fusion.1
  222.1 1.9 copy.56
  224.0 9.3 fusion.174
  238.1 2.1 fusion.171
  247.1 1.9 gather_fusion.1
  251.6 1.9 copy.56
  253.6 9.3 fusion.174
  267.7 2.1 fusion.171
  276.7 1.9 gather_fusion.1
  281.2 1.9 copy.56
  283.2 9.3 fusion.174
  297.3 2.1 fusion.171
  306.3 1.9 gather_fusion.1
  310.8 1.9 copy.56
  312.8 9.3 fusion.174
  326.9 2.1 fusion.171
  335.9 1.9 gather_fusion.1
  340.4 1.9 copy.56
  342.3 9.3 fusion.174
  356.5 2.1 fusion.171
  365.5 1.9 gather_fusion.1
  370.0 1.9 copy.56
  371.9 9.3 fusion.174
  386.1 2.1 fusion.171
  395.1 1.9 gather_fusion.1
  399.6 1.9 copy.56
  401.5 9.3 fusion.174
  415.7 2.1 fusion.171
  424.7 1.9 gather_fusion.1
  429.2 1.9 copy.56
  431.1 9.3 fusion.174
  445.3 2.1 fusion.171
  454.3 1.9 gather_fusion.1
  458.8 1.9 copy.56
  460.7 9.3 fusion.174
  474.8 2.1 fusion.171
  484.7 39.5 %all-reduce.1 = f32[8,128,8]{1,2,0:T(8,128)S(1)} all-reduce(f32[8,128,8]{1,2,0:T(8,128)S(1)} %get-tuple-element.391), channel_id=3, replica_groups=mesh['row'=8,'col'=32] {'row'}, use_global_device_ids=true, to_apply=%region_11.13.clone | all-reduce | flops 8192 | bytes 65536
  524.3 203.3 %all-reduce.8.cloned.1.call-done = f32[32,128,8]{1,2,0:T(8,128)} async-done(((f32[32,128,8]{1,2,0:T(8,128)}), f32[32,128,8]{1,2,0:T(8,128)}) %all-reduce.8.cloned.1.call-update) | async-done | bytes 131088
  727.5 2.5 multiply_convert_fusion
  730.1 39.7 %all_gather.31 = bf16[4096,8]{0,1:T(8,128)(2,1)S(1)} all-gather(bf16[128,8]{0,1:T(8,128)(2,1)S(1)} %get-tuple-element.780), channel_id=1, replica_groups=mesh['row'=8,'col'=32] {'col'}, dimensions={0}, use_global_device_ids=true | all-gather | bytes 67584 | tf_op jit(solution)/shard_map/all_gather | solution.py:164
  769.7 35.1 %all_gather.30 = bf16[1024,8]{0,1:T(8,128)(2,1)S(1)} all-gather(bf16[128,8]{0,1:T(8,128)(2,1)S(1)} %get-tuple-element.780), channel_id=1, replica_groups=mesh['row'=8,'col'=32] {'row'}, dimensions={0}, use_global_device_ids=true | all-gather | bytes 18432 | tf_op jit(solution)/shard_map/all_gather | solution.py:167
  804.8 144.6 %while.33 = (s32[]{:T(128)}, f32[32,128,8]{1,2,0:T(8,128)S(1)}, f32[8,128,8]{1,2,0:T(8,128)S(1)}, s32[]{:T(128)}, s32[256]{0:T(256)}, /*index=5*/bf16[32,128,128...) while((s32[]{:T(128)}, f32[32,128,8]{1,2,0:T(8,128)S(1)}, ...), condition=%wide.region_19.21_spmd.clone.clone, body=%wide.region_14.20_spmd.clone.clone.sunk | while | flops 205513184 | bytes 14005563 | solution.py:102
  807.8 1.9 gather_fusion.11
  823.9 1.9 gather_fusion.11
  839.9 1.9 gather_fusion.11
  855.9 1.9 gather_fusion.11
  872.0 1.9 gather_fusion.11
  888.0 1.9 gather_fusion.11
  904.1 1.9 gather_fusion.11
  920.1 1.9 gather_fusion.11
  936.1 1.9 gather_fusion.11
  950.7 45.4 %all-reduce.3 = f32[8,128,8]{1,2,0:T(8,128)S(1)} all-reduce(f32[8,128,8]{1,2,0:T(8,128)S(1)} %get-tuple-element.393), channel_id=5, replica_groups=mesh['row'=8,'col'=32] {'row'}, use_global_device_ids=true, to_apply=%region_21.23.clone | all-reduce | flops 8192 | bytes 65536
  996.1 204.5 %all-reduce.10.cloned.1.call-done = f32[32,128,8]{1,2,0:T(8,128)} async-done(((f32[32,128,8]{1,2,0:T(8,128)}), f32[32,128,8]{1,2,0:T(8,128)}) %all-reduce.10.cloned.1.call-update) | async-done | bytes 131088
  1200.6 2.1 multiply_reduce_fusion.6
  1202.7 77.4 %all-reduce.4 = (f32[8]{0:T(128)S(1)}, f32[8]{0:T(128)S(1)}, f32[8]{0:T(128)S(1)}) all-reduce(f32[8]{0:T(128)S(1)} %get-tuple-element.680, f32[8]{0:T(128)S(1)} %get-tuple-element.679, f32[8]{0:T(128)S(1)} %get-tuple-element.678), channel_id=1, replica_groups=mesh['row'=8,'col'=32] {'row','col'}, use_global_device_ids=true, to_apply=%region_13.15 | all-reduce | flops 24 | bytes 192 | tf_op jit(solution)/shard_map/psum | solution.py:178
  1280.6 2.6 multiply_subtract_fusion
  (880 shorter events, 264.3 us)
Async XLA Ops:
  7.2 205.5 %all-gather.4.cloned.1.call-start = ((), (), s32[]{:S(2)}) async-start(), calls=%async_computation | async-start | bytes 1081344 | tf_op jit(solution)/shard_map/all_gather | solution.py:137
  7.9 719.6 %all-reduce.8.cloned.1.call-start = ((), (), s32[]{:S(2)}) async-start(), calls=%async_computation.1 | async-start | bytes 262144
  217.5 1.9 copy-start.2
  224.0 10.3 copy-start.6
  224.0 10.4 copy-start.8
  237.5 0.7 copy-start.10
  240.2 3.0 copy-start.3
  247.1 1.9 copy-start.2
  253.6 10.3 copy-start.6
  253.6 10.4 copy-start.8
  267.1 0.7 copy-start.10
  269.8 3.0 copy-start.3
  276.7 1.9 copy-start.2
  283.2 10.3 copy-start.6
  283.2 10.4 copy-start.8
  296.7 0.7 copy-start.10
  299.4 3.0 copy-start.3
  306.3 1.9 copy-start.2
  312.8 10.3 copy-start.6
  312.8 10.4 copy-start.8
  326.2 0.7 copy-start.10
  329.0 3.0 copy-start.3
  335.9 1.9 copy-start.2
  342.3 10.3 copy-start.6
  342.3 10.4 copy-start.8
  355.8 0.7 copy-start.10
  358.6 3.0 copy-start.3
  365.5 1.9 copy-start.2
  371.9 10.3 copy-start.6
  371.9 10.4 copy-start.8
  385.4 0.7 copy-start.10
  388.2 3.0 copy-start.3
  395.1 1.9 copy-start.2
  401.5 10.3 copy-start.6
  401.5 10.4 copy-start.8
  417.7 3.0 copy-start.3
  424.7 1.9 copy-start.2
  431.1 10.3 copy-start.6
  431.1 10.4 copy-start.8
  444.6 0.7 copy-start.10
  447.3 3.0 copy-start.3
  454.2 1.9 copy-start.2
  460.7 10.3 copy-start.6
  460.7 10.4 copy-start.8
  476.9 3.0 copy-start.3
  481.7 718.9 %all-reduce.10.cloned.1.call-start = ((), (), s32[]{:S(2)}) async-start(), calls=%async_computation.2 | async-start | bytes 262144
  811.9 1.8 copy-start.7
  811.9 1.8 copy-start.9
  827.9 1.8 copy-start.7
  827.9 1.8 copy-start.9
  843.9 1.8 copy-start.7
  843.9 1.8 copy-start.9
  860.0 1.8 copy-start.7
  860.0 1.8 copy-start.9
  876.0 1.8 copy-start.7
  876.0 1.8 copy-start.9
  892.0 1.8 copy-start.7
  892.1 1.8 copy-start.9
  908.1 1.8 copy-start.7
  908.1 1.8 copy-start.9
  924.1 1.8 copy-start.7
  924.1 1.8 copy-start.9
  940.2 1.8 copy-start.7
  940.2 1.8 copy-start.9
  (22 other events, 13.3 us)
Sparse Core Ops, SparseCore 0:
  9.9 63.0 all-gather.3
  481.9 245.6 all-reduce.7
  950.2 250.3 all-reduce.9
where the time goes:
time: 1290 us
  blocking collectives  432 us (33%)
  waiting for transfers between devices  409 us (32%)
  other arithmetic  221 us (17%)
  local copies, waits for them, and re-layouts  183 us (14%)
  matrix products  25.4 us (2%)
  between operations  14.6 us (1%)
    unnamed x5, waiting for transfers between devices  408 us
    convert_element_type x56, other arithmetic, action_features(): jnp.where(levels == 0, constant_term, wave_terms).astype(jnp.bfloat16)  130 us
    unnamed x2, blocking collectives  84.9 us
    psum x1, blocking collectives, on_device(): lax.psum((jnp.sum(right_side * right_side, axis=0), jnp.sum(right_side *...  77.4 us
    all_gather x1, blocking collectives, on_device(): lax.all_gather(logged_actions, 'col', axis=0, tiled=True)  46.1 us
    all_gather x1, blocking collectives, on_device(): lax.all_gather(policy_actions, 'col', axis=0, tiled=True)  44.6 us
    all_gather x1, blocking collectives, on_device(): lax.all_gather(right_low, 'col', axis=0, tiled=True)  39.7 us
    all_gather x1, blocking collectives, on_device(): lax.all_gather(contexts, 'row', axis=0, tiled=True)  37.9 us
  transfers between devices with their start and end apart: 3, of which 2 were waited for; matrix products, arithmetic and copies ran while one was open for 1% of the time, Pallas kernels for 0%

commit v1 on v0

--- a/solution.py
+++ b/solution.py
@@ -12,6 +12,11 @@
 stride_base = 1009
 phase_step = 0.37
 two_pi = 2.0 * math.pi
+
+
+def axis_by_axis(value, one, other):
+    partial = lax.psum(value, one)
+    return lax.psum(partial, other)
 
 
 def action_features(chosen, width):
@@ -175,13 +180,14 @@
     )
     second_left, second_right = sweep(left_second, right_second)
     image = reduce_terms(second_left, second_right) + ridge * right_side
-    norm_sums, curvature, reward_sums = lax.psum(
+    norm_sums, curvature, reward_sums = axis_by_axis(
         (
             jnp.sum(right_side * right_side, axis=0),
             jnp.sum(right_side * image, axis=0),
             jnp.sum(rewards[:, None] * right_side, axis=0),
         ),
-        ("row", "col"),
+        "row",
+        "col",
     )
     alpha = norm_sums / curvature
     weights = alpha[None, :] * right_side

time: 1290 us -> 1310 us (1.016)
  blocking collectives: 432 us -> 455 us
    psum x1 -> x2, blocking collectives: 77.4 us -> 100 us  [the longest x1 74.2 us: axis_by_axis(): return lax.psum(partial, other)]
where the time goes in v1:
time: 1310 us
  blocking collectives  455 us (35%)
  waiting for transfers between devices  408 us (31%)
  other arithmetic  221 us (17%)
  local copies, waits for them, and re-layouts  183 us (14%)
  matrix products  25.5 us (2%)
  between operations  14.6 us (1%)
    unnamed x5, waiting for transfers between devices  408 us
    convert_element_type x56, other arithmetic, action_features(): jnp.where(levels == 0, constant_term, wave_terms).astype(jnp.bfloat16)  130 us
    unnamed x2, blocking collectives  84.9 us
    psum x1, blocking collectives, axis_by_axis(): return lax.psum(partial, other)  74.2 us
    all_gather x1, blocking collectives, on_device(): lax.all_gather(logged_actions, 'col', axis=0, tiled=True)  46.1 us
    all_gather x1, blocking collectives, on_device(): lax.all_gather(policy_actions, 'col', axis=0, tiled=True)  44.6 us
    all_gather x1, blocking collectives, on_device(): lax.all_gather(right_low, 'col', axis=0, tiled=True)  39.7 us
    all_gather x1, blocking collectives, on_device(): lax.all_gather(contexts, 'row', axis=0, tiled=True)  37.9 us
  transfers between devices with their start and end apart: 3, of which 2 were waited for; matrix products, arithmetic and copies ran while one was open for 1% of the time, Pallas kernels for 0%

profile of v1, /device:TPU:1, one launch (start us, length us, event | category | flops | bytes accessed | tf_op | source)
XLA Modules:
  0.0 1311.6 jit_solution(13944894183374665811)
XLA Ops:
  11.6 3.2 sort.19
  14.8 29.4 %all-gather.1 = s32[8,1,128]{2,1,0:T(1,128)S(1)} all-gather(s32[1,1,128]{2,1,0:T(1,128)} %bitcast.113), channel_id=1, replica_groups=mesh['row'=8,'col'=32] {'row'}, dimensions={0}, use_global_device_ids=true | all-gather | bytes 4608 | tf_op jit(solution)/shard_map/all_gather | solution.py:131
  44.2 46.1 %all-gather = s32[32,1,128]{2,1,0:T(1,128)S(1)} all-gather(s32[1,1,128]{2,1,0:T(1,128)} %bitcast.114), channel_id=1, replica_groups=mesh['row'=8,'col'=32] {'col'}, dimensions={0}, use_global_device_ids=true | all-gather | bytes 16896 | tf_op jit(solution)/shard_map/all_gather | solution.py:127
  90.3 37.4 %all_gather.26 = s32[1024,8]{0,1:T(8,128)S(1)} all-gather(s32[128,8]{0,1:T(8,128)} %param.12), channel_id=1, replica_groups=mesh['row'=8,'col'=32] {'row'}, dimensions={0}, use_global_device_ids=true | all-gather | bytes 36864 | tf_op jit(solution)/shard_map/all_gather | solution.py:132
  127.8 44.6 %all_gather.28 = s32[4096,8]{0,1:T(8,128)S(1)} all-gather(s32[128,8]{0,1:T(8,128)} %param.12), channel_id=1, replica_groups=mesh['row'=8,'col'=32] {'col'}, dimensions={0}, use_global_device_ids=true | all-gather | bytes 135168 | tf_op jit(solution)/shard_map/all_gather | solution.py:128
  173.5 37.9 %all_gather.25 = bf16[1024,128]{1,0:T(8,128)(2,1)S(1)} all-gather(bf16[128,128]{1,0:T(8,128)(2,1)} %param.10), channel_id=1, replica_groups=mesh['row'=8,'col'=32] {'row'}, dimensions={0}, use_global_device_ids=true | all-gather | bytes 294912 | tf_op jit(solution)/shard_map/all_gather | solution.py:138
  214.6 266.5 %while.32 = (s32[]{:T(128)}, f32[32,128,8]{1,2,0:T(8,128)S(1)}, f32[8,128,8]{1,2,0:T(8,128)S(1)}, s32[]{:T(128)}, s32[256]{0:T(256)}, /*index=5*/bf16[32,128,128...) while((s32[]{:T(128)}, f32[32,128,8]{1,2,0:T(8,128)S(1)}, ...), condition=%wide.region_9.11_spmd.clone.clone, body=%wide.region_4.10_spmd.clone.clone.sunk | while | flops 213377504 | bytes 27038416 | solution.py:107
  217.6 1.9 gather_fusion.1
  222.1 1.9 copy.56
  224.0 9.3 fusion.174
  238.1 2.1 fusion.171
  247.1 1.9 gather_fusion.1
  251.6 1.9 copy.56
  253.6 9.3 fusion.174
  267.7 2.1 fusion.171
  276.7 1.9 gather_fusion.1
  281.2 1.9 copy.56
  283.2 9.3 fusion.174
  297.3 2.1 fusion.171
  306.3 1.9 gather_fusion.1
  310.8 1.9 copy.56
  312.8 9.3 fusion.174
  326.9 2.1 fusion.171
  335.9 1.9 gather_fusion.1
  340.4 1.9 copy.56
  342.4 9.3 fusion.174
  356.5 2.1 fusion.171
  365.5 1.9 gather_fusion.1
  370.0 1.9 copy.56
  371.9 9.3 fusion.174
  386.1 2.1 fusion.171
  395.1 1.9 gather_fusion.1
  399.6 1.9 copy.56
  401.5 9.3 fusion.174
  415.7 2.1 fusion.171
  424.7 1.9 gather_fusion.1
  429.2 1.9 copy.56
  431.1 9.3 fusion.174
  445.3 2.1 fusion.171
  454.3 1.9 gather_fusion.1
  458.8 1.9 copy.56
  460.7 9.3 fusion.174
  474.9 2.1 fusion.171
  484.8 39.5 %all-reduce.1 = f32[8,128,8]{1,2,0:T(8,128)S(1)} all-reduce(f32[8,128,8]{1,2,0:T(8,128)S(1)} %get-tuple-element.391), channel_id=3, replica_groups=mesh['row'=8,'col'=32] {'row'}, use_global_device_ids=true, to_apply=%region_11.13.clone | all-reduce | flops 8192 | bytes 65536
  524.3 203.0 %all-reduce.9.cloned.1.call-done = f32[32,128,8]{1,2,0:T(8,128)} async-done(((f32[32,128,8]{1,2,0:T(8,128)}), f32[32,128,8]{1,2,0:T(8,128)}) %all-reduce.9.cloned.1.call-update) | async-done | bytes 131088
  727.2 2.5 multiply_convert_fusion
  729.8 39.7 %all_gather.31 = bf16[4096,8]{0,1:T(8,128)(2,1)S(1)} all-gather(bf16[128,8]{0,1:T(8,128)(2,1)S(1)} %get-tuple-element.783), channel_id=1, replica_groups=mesh['row'=8,'col'=32] {'col'}, dimensions={0}, use_global_device_ids=true | all-gather | bytes 67584 | tf_op jit(solution)/shard_map/all_gather | solution.py:169
  769.4 35.1 %all_gather.30 = bf16[1024,8]{0,1:T(8,128)(2,1)S(1)} all-gather(bf16[128,8]{0,1:T(8,128)(2,1)S(1)} %get-tuple-element.783), channel_id=1, replica_groups=mesh['row'=8,'col'=32] {'row'}, dimensions={0}, use_global_device_ids=true | all-gather | bytes 18432 | tf_op jit(solution)/shard_map/all_gather | solution.py:172
  804.5 144.3 %while.33 = (s32[]{:T(128)}, f32[32,128,8]{1,2,0:T(8,128)S(1)}, f32[8,128,8]{1,2,0:T(8,128)S(1)}, s32[]{:T(128)}, s32[256]{0:T(256)}, /*index=5*/bf16[32,128,128...) while((s32[]{:T(128)}, f32[32,128,8]{1,2,0:T(8,128)S(1)}, ...), condition=%wide.region_20.22_spmd.clone.clone, body=%wide.region_15.21_spmd.clone.clone.sunk | while | flops 205513184 | bytes 14005563 | solution.py:107
  807.5 1.9 gather_fusion.11
  823.5 1.9 gather_fusion.11
  839.6 1.9 gather_fusion.11
  855.6 1.9 gather_fusion.11
  871.6 1.9 gather_fusion.11
  887.6 1.9 gather_fusion.11
  903.6 1.9 gather_fusion.11
  919.6 1.9 gather_fusion.11
  935.6 1.9 gather_fusion.11
  950.2 45.4 %all-reduce.3 = f32[8,128,8]{1,2,0:T(8,128)S(1)} all-reduce(f32[8,128,8]{1,2,0:T(8,128)S(1)} %get-tuple-element.393), channel_id=5, replica_groups=mesh['row'=8,'col'=32] {'row'}, use_global_device_ids=true, to_apply=%region_22.24.clone | all-reduce | flops 8192 | bytes 65536
  995.5 204.0 %all-reduce.11.cloned.1.call-done = f32[32,128,8]{1,2,0:T(8,128)} async-done(((f32[32,128,8]{1,2,0:T(8,128)}), f32[32,128,8]{1,2,0:T(8,128)}) %all-reduce.11.cloned.1.call-update) | async-done | bytes 131088
  1199.6 2.1 multiply_reduce_fusion.6
  1201.7 26.0 %all-reduce.5 = (f32[8]{0:T(128)S(1)}, f32[8]{0:T(128)S(1)}, f32[8]{0:T(128)S(1)}) all-reduce(f32[8]{0:T(128)S(1)} %get-tuple-element.680, f32[8]{0:T(128)S(1)} %get-tuple-element.679, f32[8]{0:T(128)S(1)} %get-tuple-element.678), channel_id=1, replica_groups=mesh['row'=8,'col'=32] {'row'}, use_global_device_ids=true, to_apply=%region_13.15 | all-reduce | flops 24 | bytes 192 | tf_op jit(solution)/shard_map/psum | solution.py:18
  1227.7 74.2 %all-reduce.4 = (f32[8]{0:T(128)S(1)}, f32[8]{0:T(128)S(1)}, f32[8]{0:T(128)S(1)}) all-reduce(f32[8]{0:T(128)S(1)} %get-tuple-element.774, f32[8]{0:T(128)S(1)} %get-tuple-element.775, f32[8]{0:T(128)S(1)} %get-tuple-element.776), channel_id=1, replica_groups=mesh['row'=8,'col'=32] {'col'}, use_global_device_ids=true, to_apply=%region_14.16 | all-reduce | flops 24 | bytes 192 | tf_op jit(solution)/shard_map/psum | solution.py:19
  1302.4 2.6 multiply_subtract_fusion
  (881 shorter events, 265.9 us)
Async XLA Ops:
  7.2 205.5 %all-gather.4.cloned.1.call-start = ((), (), s32[]{:S(2)}) async-start(), calls=%async_computation | async-start | bytes 1081344 | tf_op jit(solution)/shard_map/all_gather | solution.py:142
  7.9 719.4 %all-reduce.9.cloned.1.call-start = ((), (), s32[]{:S(2)}) async-start(), calls=%async_computation.1 | async-start | bytes 262144
  217.5 1.9 copy-start.2
  224.0 10.3 copy-start.6
  224.0 10.4 copy-start.8
  237.5 0.7 copy-start.10
  240.2 3.0 copy-start.3
  247.1 1.9 copy-start.2
  253.6 10.3 copy-start.6
  253.6 10.4 copy-start.8
  267.1 0.7 copy-start.10
  269.8 3.0 copy-start.3
  276.7 1.9 copy-start.2
  283.2 10.3 copy-start.6
  283.2 10.4 copy-start.8
  299.4 3.0 copy-start.3
  306.3 1.9 copy-start.2
  312.8 10.3 copy-start.6
  312.8 10.4 copy-start.8
  329.0 3.0 copy-start.3
  335.9 1.9 copy-start.2
  342.3 10.4 copy-start.6
  342.4 10.4 copy-start.8
  355.8 0.7 copy-start.10
  358.6 3.0 copy-start.3
  365.5 1.9 copy-start.2
  371.9 10.3 copy-start.6
  371.9 10.4 copy-start.8
  385.4 0.7 copy-start.10
  388.2 3.0 copy-start.3
  395.1 1.9 copy-start.2
  401.5 10.3 copy-start.6
  401.5 10.4 copy-start.8
  415.0 0.7 copy-start.10
  417.8 3.0 copy-start.3
  424.7 1.9 copy-start.2
  431.1 10.3 copy-start.6
  431.1 10.4 copy-start.8
  444.6 0.7 copy-start.10
  447.4 3.0 copy-start.3
  454.3 1.9 copy-start.2
  460.7 10.4 copy-start.6
  460.7 10.4 copy-start.8
  474.2 0.7 copy-start.10
  476.9 3.0 copy-start.3
  481.8 717.8 %all-reduce.11.cloned.1.call-start = ((), (), s32[]{:S(2)}) async-start(), calls=%async_computation.2 | async-start | bytes 262144
  811.6 1.7 copy-start.7
  811.6 1.7 copy-start.9
  827.6 1.7 copy-start.7
  827.6 1.7 copy-start.9
  843.6 1.7 copy-start.7
  843.6 1.7 copy-start.9
  859.6 1.7 copy-start.7
  859.6 1.7 copy-start.9
  875.6 1.7 copy-start.7
  875.6 1.7 copy-start.9
  891.6 1.7 copy-start.7
  891.6 1.7 copy-start.9
  907.6 1.7 copy-start.7
  907.6 1.7 copy-start.9
  923.6 1.7 copy-start.7
  923.6 1.7 copy-start.9
  939.6 1.7 copy-start.7
  939.6 1.7 copy-start.9
  (22 other events, 13.3 us)
Sparse Core Ops, SparseCore 0:
  9.9 63.0 all-gather.3
  481.9 245.3 all-reduce.8
  949.6 249.9 all-reduce.10
